TPU v7x, 32 devices: a whole 2x2x4 slice. The times are simulated.
32 devices in a mesh: grp: 2 (over x), chol: 16 (over z, y, core).
Axes of the slice: x: 2, y: 2, z: 4, core: 2. Of those that a mesh axis runs over, the one named last changes fastest.
Arguments:
- chol_full: bfloat16 [128, 1024, 1024], P(None, 'chol'), may hold values from -0.015625 to 0.015625
- chol_half: bfloat16 [128, 1024, 256], P(None, 'chol'), may hold values from -0.046875 to 0.046875
- green: bfloat16 [128, 1024, 256], P('grp', 'chol'), parts along dimension 0, may hold values from -6 to 6
- gauss: float32 [128, 128], P('grp'), parts along dimension 0, may hold values from -5 to 5
- orbitals: bfloat16 [128, 1024, 256], P(('grp', 'chol')), parts along dimension 0, may hold values from -6 to 6
Outputs:
- new_orbitals: bfloat16 [128, 1024, 256], P(('grp', 'chol')), parts along dimension 0
- log_factor: float32 [128], P(('grp', 'chol')), parts along dimension 0
There are 2 independent parts, one for each index of `grp`. A program takes and returns all parts, laid end to end along the dimension named above; an argument that names none is the same for every part. Nothing has to cross between parts.
All inputs are finite; a program needn't handle non-finite values.
Results may differ from a plain program's by a relative error of at most 0.0032.
Values may be sent and summed in bfloat16 or wider, within the bound.
A program may use at most 128 MiB of HBM per device.

v0:
```python
import jax
import jax.numpy as jnp
from jax import lax
from jax.sharding import PartitionSpec as P


def shift_terms(vbias, gauss_rows):
    xbar = jnp.clip(-0.3 * vbias, -1.0, 1.0)
    log_terms = jnp.sum(gauss_rows * xbar - 0.5 * xbar * xbar, axis=1)
    fields = (gauss_rows - xbar).astype(jnp.bfloat16)
    return (fields, log_terms)


def on_device(chol_full, chol_half, green, gauss, orbitals):
    walkers = green.shape[0]
    local_rows = green.shape[1]
    owned = orbitals.shape[0]
    vectors = chol_half.shape[0]
    partial_value = lax.dot_general(
        green.reshape(walkers, -1),
        chol_half.reshape(vectors, -1),
        (((1,), (1,)), ((), ())),
        preferred_element_type=jnp.float32,
    )
    first = lax.axis_index("chol") * owned
    vbias = lax.psum(partial_value, "chol")
    fields, log_terms = shift_terms(vbias, gauss)
    log_factor = lax.dynamic_slice_in_dim(log_terms, first, owned, 0)
    width = chol_full.shape[2]
    potential = jnp.dot(
        fields, chol_full.reshape(vectors, local_rows * width), preferred_element_type=jnp.float32
    )
    potential = (potential * 0.3).astype(jnp.bfloat16).reshape(walkers, local_rows, width)
    whole = lax.all_to_all(potential, "chol", split_axis=0, concat_axis=1, tiled=True)
    moved = jnp.einsum("wpq,wqk->wpk", whole, orbitals, preferred_element_type=jnp.float32)
    new_orbitals = (orbitals.astype(jnp.float32) + moved).astype(jnp.bfloat16)
    return (new_orbitals, log_factor)


def solution(mesh):
    placed = (
        P(None, "chol", None),
        P(None, "chol", None),
        P("grp", "chol", None),
        P("grp", None),
        P(("grp", "chol"), None, None),
    )
    return jax.shard_map(
        on_device,
        mesh=mesh,
        in_specs=placed,
        out_specs=(P(("grp", "chol"), None, None), P(("grp", "chol"))),
        check_vma=False,
    )
```

profile of v0, /device:TPU:13, one launch (start us, length us, event | category | flops | bytes accessed | tf_op | source)
XLA Modules:
  0.0 314.3 jit_solution(14263485968305415056)
XLA Ops:
  0.6 0.0 copy-start.1
  0.6 0.0 copy-start.2
  0.6 18.8 %copy.10 = bf16[16,8,64,1024]{3,1,2,0:T(8,128)(2,1)} copy(bf16[16,8,64,1024]{3,2,1,0:T(8,128)(2,1)} %bitcast.16) | data formatting | bytes 33554432
  19.5 0.0 copy-done.1
  19.5 0.0 copy-done.2
  19.5 0.0 copy-start
  19.5 6.7 %fusion.4 = f32[64,128]{1,0:T(8,128)S(1)} fusion(bf16[128,64,256]{2,1,0:T(8,128)(2,1)S(1)} %copy-done.1, bf16[64,64,256]{2,1,0:T(8,128)(2,1)S(1)} %copy-done.2), kind=kOutput, calls=%fused_computation.6 | convolution fusion | flops 268435456 | bytes 6324224 | tf_op jit(solution)/shard_map/dot_general | solution.py:19
  26.2 44.7 %psum.7 = f32[64,128]{1,0:T(8,128)S(1)} all-reduce(f32[64,128]{1,0:T(8,128)S(1)} %fusion.4), channel_id=1, replica_groups=mesh['grp'=2,'chol'=16] {'chol'}, use_global_device_ids=true, to_apply=%region_0.0 | all-reduce | flops 8192 | bytes 65536 | tf_op jit(solution)/shard_map/psum | solution.py:26
  70.8 0.0 copy-done
  70.8 11.8 %fusion = bf16[64,65536]{1,0:T(8,128)(2,1)} fusion(bf16[128,65536]{1,0:T(8,128)(2,1)} %bitcast.13, f32[64,128]{1,0:T(8,128)S(1)} %copy-done, f32[64,128]{1,0:T(8,128)S(1)} %psum.7), kind=kOutput, calls=%fused_computation.1 | convolution fusion | flops 1082163200 | bytes 25231360 | tf_op jit(solution)/shard_map/dot_general | solution.py:30
  82.6 11.6 %copy.11 = bf16[8,8,64,1024]{3,2,1,0:T(8,128)(2,1)} copy(bf16[8,8,64,1024]{3,1,2,0:T(8,128)(2,1)} %bitcast.14) | data formatting | bytes 16777216
  94.2 22.0 %all-to-all-start = ((bf16[64,64,1024]{2,1,0:T(8,128)(2,1)}), bf16[64,64,1024]{2,1,0:T(8,128)(2,1)}, u32[]{:S(2)}, u32[]{:S(2)}) async-start(bf16[64,64,1024]{2,1,0:T(8,128)(2,1)} %bitcast.15), calls=%async_computation | async-start | bytes 16777216 | tf_op jit(solution)/shard_map/all_to_all | solution.py:34
  116.2 0.1 fusion.10
  116.4 0.6 dynamic_slice.3
  117.0 181.7 %all-to-all-done = bf16[64,64,1024]{2,1,0:T(8,128)(2,1)} async-done(((bf16[64,64,1024]{2,1,0:T(8,128)(2,1)}), bf16[64,64,1024]{2,1,0:T(8,128)(2,1)}, u32[]{:S(2)}, u32[]{:S(2)}) %all-to-all-start) | async-done | bytes 8388640 | tf_op jit(solution)/shard_map/all_to_all | solution.py:34
  298.6 0.0 copy-start.3
  298.6 8.5 %copy.9 = bf16[16,4,64,1024]{3,2,0,1:T(8,128)(2,1)} copy(bf16[16,4,64,1024]{3,2,1,0:T(8,128)(2,1)} %bitcast.1) | data formatting | bytes 16777216 | tf_op jit(solution)/shard_map/all_to_all | solution.py:34
  307.2 0.0 copy-done.3
  307.2 7.1 %add_convert_fusion = bf16[4,1024,256]{2,1,0:T(8,128)(2,1)} fusion(bf16[4,1024,256]{2,1,0:T(8,128)(2,1)S(1)} %copy-done.3, bf16[4,1024,1024]{2,1,0:T(8,128)(2,1)} %bitcast.17), kind=kOutput, calls=%fused_computation.4 | convolution fusion | flops 2150629376 | bytes 12582912 | tf_op jit(solution)/shard_map/wpq,wqk->wpk/dot_general | solution.py:35
Async XLA Ops:
  0.6 18.8 %copy-start.1 = (bf16[128,64,256]{2,1,0:T(8,128)(2,1)S(1)}, bf16[128,64,256]{2,1,0:T(8,128)(2,1)}, u32[]{:S(2)}) copy-start(bf16[128,64,256]{2,1,0:T(8,128)(2,1)} %param.6) | copy-start | bytes 12582916
  0.6 18.8 %copy-start.2 = (bf16[64,64,256]{2,1,0:T(8,128)(2,1)S(1)}, bf16[64,64,256]{2,1,0:T(8,128)(2,1)}, u32[]{:S(2)}) copy-start(bf16[64,64,256]{2,1,0:T(8,128)(2,1)} %param.7) | copy-start | bytes 6291460
  19.5 51.4 %copy-start = (f32[64,128]{1,0:T(8,128)S(1)}, f32[64,128]{1,0:T(8,128)}, u32[]{:S(2)}) copy-start(f32[64,128]{1,0:T(8,128)} %param.8) | copy-start | bytes 98308
  94.2 204.4 %all-to-all-start = ((bf16[64,64,1024]{2,1,0:T(8,128)(2,1)}), bf16[64,64,1024]{2,1,0:T(8,128)(2,1)}, u32[]{:S(2)}, u32[]{:S(2)}) async-start(bf16[64,64,1024]{2,1,0:T(8,128)(2,1)} %bitcast.15), calls=%async_computation | async-start | bytes 16777216 | tf_op jit(solution)/shard_map/all_to_all | solution.py:34
  298.6 8.5 %copy-start.3 = (bf16[4,1024,256]{2,1,0:T(8,128)(2,1)S(1)}, bf16[4,1024,256]{2,1,0:T(8,128)(2,1)}, u32[]{:S(2)}) copy-start(bf16[4,1024,256]{2,1,0:T(8,128)(2,1)} %param.9) | copy-start | bytes 6291460
where the time goes:
time: 315 us; the launch traced here: 314 us
  waiting for transfers between devices  182 us (58%)
  blocking collectives  44.7 us (14%)
  local copies, waits for them, and re-layouts  39.6 us (13%)
  matrix products  25.5 us (8%)
  starting transfers between devices  22 us (7%)
    all_to_all x1, waiting for transfers between devices, on_device(): lax.all_to_all(potential, 'chol', split_axis=0, concat_axis=1, tiled=True)  182 us
    psum x1, blocking collectives, on_device(): vbias = lax.psum(partial_value, 'chol')  44.7 us
    unnamed x10, local copies, waits for them, and re-layouts  30.4 us
    all_to_all x1, starting transfers between devices, on_device(): lax.all_to_all(potential, 'chol', split_axis=0, concat_axis=1, tiled=True)  22 us
    dot_general x1, matrix products, on_device(): jnp.dot(fields, chol_full.reshape(vectors, local_rows * width), preferred...  11.8 us
    all_to_all x1, local copies, waits for them, and re-layouts, on_device(): lax.all_to_all(potential, 'chol', split_axis=0, concat_axis=1, tiled=True)  8.54 us
    dot_general x1, matrix products, on_device(): jnp.einsum('wpq,wqk->wpk', whole, orbitals, preferred_element_type=jnp.fl...  7.1 us
    dot_general x1, matrix products, on_device(): lax.dot_general(green.reshape(walkers, -1), chol_half.reshape(vectors, -1...  6.68 us
  transfers between devices with their start and end apart: 1, of which 1 were waited for; matrix products, arithmetic and copies ran while one was open for 0% of the time, Pallas kernels for 0%

commit v1 on v0

v1 whole, which is shorter than its diff:
```python
import functools

import jax
import jax.numpy as jnp
from jax import lax
from jax.experimental import pallas as pl
from jax.experimental.pallas import tpu as pltpu
from jax.sharding import PartitionSpec as P

TILE = 16
LANES = 128


def remote(src, dst, send, recv, peer):
    return pltpu.make_async_remote_copy(
        src_ref=src,
        dst_ref=dst,
        send_sem=send,
        recv_sem=recv,
        device_id={"chol": peer},
        device_id_type=pl.DeviceIdType.MESH,
    )


def kernel(
    n, chol_hbm, half_hbm, green_hbm, gauss_ref, orb_ref,
    out_ref, log_ref,
    chol, half, green, part, part_in, fields_own, fields_in, send, recv,
    load_sem, aux_sem, part_send, part_recv, field_send, field_recv, pot_send, pot_recv,
):
    me = lax.axis_index("chol")
    owned = part.shape[1]
    tiles = chol.shape[0]
    width = chol.shape[3]

    half_copy = pltpu.make_async_copy(half_hbm, half, aux_sem.at[0])
    green_copy = pltpu.make_async_copy(green_hbm, green, aux_sem.at[1])
    half_copy.start()
    green_copy.start()
    loads = [
        pltpu.make_async_copy(chol_hbm.at[:, pl.ds(t * TILE, TILE), :], chol.at[t], load_sem.at[t])
        for t in range(tiles)
    ]
    for load in loads:
        load.start()

    barrier = pltpu.get_barrier_semaphore()

    def greet(k, _):
        pl.semaphore_signal(
            barrier, inc=1, device_id={"chol": lax.rem(me + k, n)}, device_id_type=pl.DeviceIdType.MESH
        )
        return 0

    lax.fori_loop(1, n, greet, 0)

    half_copy.wait()
    green_copy.wait()

    def bias(t, acc):
        rows = pl.ds(pl.multiple_of(t * TILE, TILE), TILE)
        left = jnp.swapaxes(green[:, rows, :], 0, 1)
        right = jnp.swapaxes(half[:, rows, :], 0, 1)
        for r in range(TILE):
            acc += lax.dot_general(
                left[r], right[r], (((1,), (1,)), ((), ())), preferred_element_type=jnp.float32
            )
        return acc

    total = lax.fori_loop(0, tiles, bias, jnp.zeros((n * owned, half.shape[0]), jnp.float32))
    for d in range(n):
        part[d] = total[d * owned:(d + 1) * owned]
    pl.semaphore_wait(barrier, n - 1)

    def peer_of(k):
        return lax.rem(me + k, n)

    def push_part(k, _):
        to = peer_of(k)
        remote(part.at[to], part_in.at[me], part_send.at[to], part_recv.at[me], to).start()
        return 0

    lax.fori_loop(1, n, push_part, 0)
    part_in[me] = part[me]

    def wait_part(k, _):
        peer = peer_of(k)
        copy = remote(part.at[peer], part_in.at[peer], part_send.at[peer], part_recv.at[peer], peer)
        copy.wait_recv()
        return 0

    lax.fori_loop(1, n, wait_part, 0)
    vbias = jnp.sum(part_in[...], axis=0)
    gauss = gauss_ref[me]
    xbar = jnp.clip(-0.3 * vbias, -1.0, 1.0)
    log_ref[...] = jnp.broadcast_to(
        jnp.sum(gauss * xbar - 0.5 * xbar * xbar, axis=1, keepdims=True), log_ref.shape
    )
    mine = gauss - xbar
    fields_own[...] = mine
    fields_in[me] = mine

    def push_field(k, _):
        to = peer_of(k)
        remote(fields_own, fields_in.at[me], field_send.at[to], field_recv.at[me], to).start()
        return 0

    lax.fori_loop(1, n, push_field, 0)

    def wait_field(k, _):
        peer = peer_of(k)
        remote(fields_own, fields_in.at[peer], field_send.at[peer], field_recv.at[peer], peer).wait_recv()
        return 0

    lax.fori_loop(1, n, wait_field, 0)
    fields = jnp.concatenate([fields_in[d] for d in range(n)], axis=0).astype(jnp.bfloat16)

    def walkers_of(d):
        return pl.ds(d * owned, owned)

    def rows_of(d):
        return pl.ds(pl.multiple_of(d * TILE, TILE), TILE)

    for t in range(tiles):
        loads[t].wait()

        def strip(c, _):
            cols = pl.ds(pl.multiple_of(c * LANES, LANES), LANES)
            block = jnp.swapaxes(chol[t, :, :, cols], 0, 1)
            pots = [
                (jnp.dot(fields, block[r], preferred_element_type=jnp.float32) * 0.3).astype(jnp.bfloat16)
                for r in range(TILE)
            ]
            send[t, :, :, cols] = jnp.swapaxes(jnp.stack(pots, axis=0), 0, 1)
            return 0

        lax.fori_loop(0, width // LANES, strip, 0)

        def push_pot(k, _):
            to = peer_of(k)
            remote(
                send.at[t, walkers_of(to)], recv.at[t, :, rows_of(me), :],
                pot_send.at[t, to], pot_recv.at[t, me], to,
            ).start()
            return 0

        lax.fori_loop(1, n, push_pot, 0)
        recv[t, :, rows_of(me), :] = send[t, walkers_of(me)]

    for t in range(tiles):

        def wait_pot(k, _):
            peer = peer_of(k)
            remote(
                send.at[t, walkers_of(peer)], recv.at[t, :, rows_of(peer), :],
                pot_send.at[t, peer], pot_recv.at[t, peer], peer,
            ).wait_recv()
            return 0

        lax.fori_loop(1, n, wait_pot, 0)

        def advance(w, _):
            orbit = orb_ref[w].reshape(width, orb_ref.shape[-1])
            for first in range(0, n, 16):
                span = min(16, n - first)
                moved = jnp.dot(
                    recv[t, w, first * TILE:(first + span) * TILE, :], orbit,
                    preferred_element_type=jnp.float32,
                ).reshape(span, TILE, orbit.shape[-1])
                old = orb_ref[w, first:first + span, t].astype(jnp.float32)
                out_ref[w, first:first + span, t] = (old + moved).astype(jnp.bfloat16)
            return 0

        lax.fori_loop(0, owned, advance, 0)

    def drain(k, _):
        peer = peer_of(k)
        remote(part.at[peer], part_in.at[peer], part_send.at[peer], part_recv.at[peer], peer).wait_send()
        remote(fields_own, fields_in.at[peer], field_send.at[peer], field_recv.at[peer], peer).wait_send()
        for t in range(tiles):
            remote(
                send.at[t, walkers_of(peer)], recv.at[t, :, rows_of(peer), :],
                pot_send.at[t, peer], pot_recv.at[t, peer], peer,
            ).wait_send()
        return 0

    lax.fori_loop(1, n, drain, 0)


def on_device(n, chol_full, chol_half, green, gauss, orbitals):
    walkers, local_rows, nocc = green.shape
    owned, width, _ = orbitals.shape
    vectors = chol_half.shape[0]
    tiles = local_rows // TILE
    vmem = pl.BlockSpec(memory_space=pltpu.VMEM)
    hbm = pl.BlockSpec(memory_space=pl.ANY)
    dma = pltpu.SemaphoreType.DMA
    split = (owned, n, tiles, TILE, nocc)
    moved, logs = pl.pallas_call(
        functools.partial(kernel, n),
        out_shape=(
            jax.ShapeDtypeStruct(split, jnp.bfloat16),
            jax.ShapeDtypeStruct((owned, LANES), jnp.float32),
        ),
        in_specs=[hbm, hbm, hbm, vmem, vmem],
        out_specs=(vmem, vmem),
        scratch_shapes=[
            pltpu.VMEM((tiles, vectors, TILE, width), jnp.bfloat16),
            pltpu.VMEM((vectors, local_rows, nocc), jnp.bfloat16),
            pltpu.VMEM((walkers, local_rows, nocc), jnp.bfloat16),
            pltpu.VMEM((n, owned, vectors), jnp.float32),
            pltpu.VMEM((n, owned, vectors), jnp.float32),
            pltpu.VMEM((owned, vectors), jnp.float32),
            pltpu.VMEM((n, owned, vectors), jnp.float32),
            pltpu.VMEM((tiles, walkers, TILE, width), jnp.bfloat16),
            pltpu.VMEM((tiles, owned, n * TILE, width), jnp.bfloat16),
            dma((tiles,)), dma((2,)), dma((n,)), dma((n,)), dma((n,)), dma((n,)),
            dma((tiles, n)), dma((tiles, n)),
        ],
        compiler_params=pltpu.CompilerParams(
            collective_id=0, has_side_effects=True, vmem_limit_bytes=60 << 20
        ),
    )(chol_full, chol_half, green, gauss.reshape(n, owned, vectors), orbitals.reshape(split))
    return moved.reshape(orbitals.shape), logs[:, 0]


def solution(mesh):
    placed = (
        P(None, "chol", None),
        P(None, "chol", None),
        P("grp", "chol", None),
        P("grp", None),
        P(("grp", "chol"), None, None),
    )
    return jax.shard_map(
        functools.partial(on_device, mesh.shape["chol"]),
        mesh=mesh,
        in_specs=placed,
        out_specs=(P(("grp", "chol"), None, None), P(("grp", "chol"))),
        check_vma=False,
    )
```

time: 315 us -> 215 us (0.68)
  Pallas kernels: 0 us -> 210 us
  waiting for transfers between devices: 182 us -> 0 us
  blocking collectives: 44.7 us -> 0 us
  local copies, waits for them, and re-layouts: 39.6 us -> 4.36 us
  matrix products: 25.5 us -> 0 us
  starting transfers between devices: 22 us -> 0 us
    pallas_call x0 -> x1, Pallas kernels: none -> 210 us  [on_device(): pl.pallas_call(functools.partial(kernel, n), out_shape=(jax.ShapeDtypeStr...]
    all_to_all x1 -> x0, waiting for transfers between devices: 182 us -> none  [on_device(): lax.all_to_all(potential, 'chol', split_axis=0, concat_axis=1, tiled=True)]
    psum x1 -> x0, blocking collectives: 44.7 us -> none  [on_device(): vbias = lax.psum(partial_value, 'chol')]
    unnamed x10 -> x1, local copies, waits for them, and re-layouts: 30.4 us -> 3.04 us
    dot_general x3 -> x0, matrix products: 25.5 us -> none  [the longest x1 11.8 us: on_device(): jnp.dot(fields, chol_full.reshape(vectors, local_rows * width), preferred...]
    all_to_all x1 -> x0, starting transfers between devices: 22 us -> none  [on_device(): lax.all_to_all(potential, 'chol', split_axis=0, concat_axis=1, tiled=True)]
    all_to_all x1 -> x0, local copies, waits for them, and re-layouts: 8.54 us -> none  [on_device(): lax.all_to_all(potential, 'chol', split_axis=0, concat_axis=1, tiled=True)]
  transfers between devices with their start and end apart: 1 -> 0, of which waited for: 1 -> 0; matrix products, arithmetic and copies ran while one was open for 0% -> 0% of each run, Pallas kernels for 0% -> 0%
where the time goes in v1:
time: 215 us
  Pallas kernels  210 us (98%)
  local copies, waits for them, and re-layouts  4.36 us (2%)
    pallas_call x1, Pallas kernels, on_device(): pl.pallas_call(functools.partial(kernel, n), out_shape=(jax.ShapeDtypeStr...  210 us

profile of v1, /device:TPU:13, one launch (start us, length us, event | category | flops | bytes accessed | tf_op | source)
XLA Modules:
  0.0 214.8 jit_solution(12214448775136527389)
XLA Ops:
  0.6 209.8 %shard_map.68 = (bf16[4,16,4,16,256]{4,3,2,1,0:T(8,128)(2,1)}, f32[4,128]{1,0:T(4,128)}) custom-call(bf16[128,64,1024]{2,1,0:T(8,128)(2,1)} %chol_hbm.1, bf16[128,64,256]{2,1,0:T(8,128)(2,1)} %half_hbm.1, bf16[64,64,256]{2,1,0:T(8,128)(2,1)} %green_hbm.1, f32[16,4,128]{2,1,0:T(4,128)} %bitcast.5, bf16[4,16,4,16,256]{4,3,2,1,0:T(8,128)(2,1)} %bitcast.3), custom_call_target="tpu_custom_call" | custom-call | tf_op jit(solution)/shard_map/pallas_call | solution.py:199
  210.5 1.3 slice_reduce_fusion
  211.8 3.0 %copy.8 = bf16[4,1024,256]{2,1,0:T(8,128)(2,1)} copy(bf16[4,1024,256]{2,1,0:T(8,128)(2,1)} %bitcast.4) | data formatting | bytes 4194304

commit v2 on v1

--- a/solution.py
+++ b/solution.py
@@ -9,6 +9,8 @@
 
 TILE = 16
 LANES = 128
+PLANE = 4
+GUEST_LIMIT = 16 << 20
 
 
 def remote(src, dst, send, recv, peer):
@@ -22,7 +24,7 @@
     )
 
 
-def kernel(
+def direct_kernel(
     n, chol_hbm, half_hbm, green_hbm, gauss_ref, orb_ref,
     out_ref, log_ref,
     chol, half, green, part, part_in, fields_own, fields_in, send, recv,
@@ -187,6 +189,283 @@
     lax.fori_loop(1, n, drain, 0)
 
 
+def relay_kernel(
+    n, chol_hbm, half_hbm, green_hbm, gauss_ref, orb_ref,
+    out_ref, log_ref,
+    chol, half, green, part, part_in, fields_own, fields_in, send, recv, guest, done,
+    load_sem, aux_sem, part_send, part_recv, field_send, field_recv, pot_send, pot_recv,
+    own_send, guest_recv, relay_send, pass_send, done_send, done_recv,
+):
+    me = lax.axis_index("chol")
+    owned = part.shape[1]
+    tiles = chol.shape[0]
+    width = chol.shape[3]
+
+    half_copy = pltpu.make_async_copy(half_hbm, half, aux_sem.at[0])
+    green_copy = pltpu.make_async_copy(green_hbm, green, aux_sem.at[1])
+    half_copy.start()
+    green_copy.start()
+    loads = [
+        pltpu.make_async_copy(chol_hbm.at[:, pl.ds(t * TILE, TILE), :], chol.at[t], load_sem.at[t])
+        for t in range(tiles)
+    ]
+    for load in loads:
+        load.start()
+
+    barrier = pltpu.get_barrier_semaphore()
+
+    def greet(k, _):
+        pl.semaphore_signal(
+            barrier, inc=1, device_id={"chol": lax.rem(me + k, n)}, device_id_type=pl.DeviceIdType.MESH
+        )
+        return 0
+
+    lax.fori_loop(1, n, greet, 0)
+
+    half_copy.wait()
+    green_copy.wait()
+
+    def bias(t, acc):
+        rows = pl.ds(pl.multiple_of(t * TILE, TILE), TILE)
+        left = jnp.swapaxes(green[:, rows, :], 0, 1)
+        right = jnp.swapaxes(half[:, rows, :], 0, 1)
+        for r in range(TILE):
+            acc += lax.dot_general(
+                left[r], right[r], (((1,), (1,)), ((), ())), preferred_element_type=jnp.float32
+            )
+        return acc
+
+    total = lax.fori_loop(0, tiles, bias, jnp.zeros((n * owned, half.shape[0]), jnp.float32))
+    for d in range(n):
+        part[d] = total[d * owned:(d + 1) * owned]
+    pl.semaphore_wait(barrier, n - 1)
+
+    def peer_of(k):
+        return lax.rem(me + k, n)
+
+    def push_part(k, _):
+        to = peer_of(k)
+        remote(part.at[to], part_in.at[me], part_send.at[to], part_recv.at[me], to).start()
+        return 0
+
+    lax.fori_loop(1, n, push_part, 0)
+    part_in[me] = part[me]
+
+    def wait_part(k, _):
+        peer = peer_of(k)
+        copy = remote(part.at[peer], part_in.at[peer], part_send.at[peer], part_recv.at[peer], peer)
+        copy.wait_recv()
+        return 0
+
+    lax.fori_loop(1, n, wait_part, 0)
+    vbias = jnp.sum(part_in[...], axis=0)
+    gauss = gauss_ref[me]
+    xbar = jnp.clip(-0.3 * vbias, -1.0, 1.0)
+    log_ref[...] = jnp.broadcast_to(
+        jnp.sum(gauss * xbar - 0.5 * xbar * xbar, axis=1, keepdims=True), log_ref.shape
+    )
+    mine = gauss - xbar
+    fields_own[...] = mine
+    fields_in[me] = mine
+
+    def push_field(k, _):
+        to = peer_of(k)
+        remote(fields_own, fields_in.at[me], field_send.at[to], field_recv.at[me], to).start()
+        return 0
+
+    lax.fori_loop(1, n, push_field, 0)
+
+    def wait_field(k, _):
+        peer = peer_of(k)
+        remote(fields_own, fields_in.at[peer], field_send.at[peer], field_recv.at[peer], peer).wait_recv()
+        return 0
+
+    lax.fori_loop(1, n, wait_field, 0)
+    fields = jnp.concatenate([fields_in[d] for d in range(n)], axis=0).astype(jnp.bfloat16)
+
+    def walkers_of(d):
+        return pl.ds(d * owned, owned)
+
+    def rows_of(d):
+        return pl.ds(pl.multiple_of(d * TILE, TILE), TILE)
+
+    near = n // 2
+    planes = near // PLANE
+    mine_at = lax.rem(me, near)
+    home = me - mine_at
+    away = near - home
+    seat = lax.rem(me, PLANE)
+    across = lax.rem(seat + 2, PLANE)
+    upper = me // near
+    entry = away + (1 - upper) * 0 + upper * (near - PLANE) + seat
+    depth = upper * (mine_at // PLANE) + (1 - upper) * (planes - 1 - mine_at // PLANE)
+    outward = lax.rem(me + n + (2 * upper - 1) * PLANE, n)
+    partner = me + 1 - 2 * lax.rem(me, 2)
+    beside = me - seat + across
+
+    def swap(j):
+        return j + 1 - 2 * lax.rem(j, 2)
+
+    def guest_copy(slot, w, sem, to):
+        return remote(guest.at[slot, w], guest.at[slot, w], sem, guest_recv.at[slot, w], to)
+
+    def host(w):
+        return remote(orb_ref.at[w], guest.at[mine_at, w], own_send.at[w], guest_recv.at[mine_at, w], entry)
+
+    for w in range(owned):
+        host(w).start()
+
+    def fill(t):
+        loads[t].wait()
+
+        def strip(c, _):
+            cols = pl.ds(pl.multiple_of(c * LANES, LANES), LANES)
+            block = jnp.swapaxes(chol[t, :, :, cols], 0, 1)
+            pots = [
+                (jnp.dot(fields, block[r], preferred_element_type=jnp.float32) * 0.3).astype(jnp.bfloat16)
+                for r in range(TILE)
+            ]
+            send[t, :, :, cols] = jnp.swapaxes(jnp.stack(pots, axis=0), 0, 1)
+            return 0
+
+        lax.fori_loop(0, width // LANES, strip, 0)
+        recv[t, :, rows_of(mine_at), :] = send[t, walkers_of(me)]
+
+    def fellow(k):
+        return lax.rem(mine_at + k, near)
+
+    def pot_copy(t, there, source):
+        return remote(
+            send.at[t, walkers_of(home + there)], recv.at[t, :, rows_of(source), :],
+            pot_send.at[t, there], pot_recv.at[t, source], home + there,
+        )
+
+    def push(t):
+        def step(k, _):
+            pot_copy(t, fellow(k), mine_at).start()
+            return 0
+
+        lax.fori_loop(1, near, step, 0)
+
+    def column(oz):
+        return oz * PLANE + seat
+
+    def relay(w):
+        for oz in range(planes):
+            slot = column(oz)
+            guest_copy(slot, w, own_send.at[w], partner).wait_recv()
+
+            @pl.when(depth < planes - 1)
+            def _():
+                guest_copy(slot, w, relay_send.at[0, oz, w], outward).start()
+
+            guest_copy(slot, w, relay_send.at[1, oz, w], beside).start()
+            guest_copy(slot, w, relay_send.at[2, oz, w], partner).start()
+
+    def hand_over(w):
+        for oz in range(planes):
+            slot = oz * PLANE + across
+            guest_copy(slot, w, own_send.at[w], partner).wait_recv()
+            guest_copy(slot, w, pass_send.at[oz, w], partner).start()
+
+    def done_copy(slot, w):
+        return remote(
+            done.at[slot, w], out_ref.at[w, me], done_send.at[slot, w], done_recv.at[mine_at, w], away + slot
+        )
+
+    def serve(slot, w):
+        left = send[:, (away + slot) * owned + w].reshape(tiles * TILE, width)
+        orbit = guest[slot, w].reshape(width, guest.shape[-1])
+        moved = jnp.dot(left, orbit, preferred_element_type=jnp.float32)
+        old = guest[slot, w, me].astype(jnp.float32)
+        done[slot, w] = (old + moved.reshape(old.shape)).astype(jnp.bfloat16)
+        done_copy(slot, w).start()
+
+    def serve_column(w, j, wait):
+        for oz in range(planes):
+            slot = oz * PLANE + j
+            if wait:
+                guest_copy(slot, w, own_send.at[w], partner).wait_recv()
+            serve(slot, w)
+
+    for t in range(tiles):
+        fill(t)
+        if t == 0:
+            push(0)
+    for w in range(owned + 1):
+        if w < owned:
+            relay(w)
+        if w == owned - 1 or (w < owned and w + 1 >= tiles):
+            for t in range(w + 1, tiles):
+                push(t)
+        elif w < owned:
+            push(w + 1)
+        if w > 0:
+            hand_over(w - 1)
+        if w < owned:
+            serve_column(w, seat, False)
+            serve_column(w, swap(seat), True)
+        if w > 0:
+            serve_column(w - 1, across, False)
+            serve_column(w - 1, swap(across), True)
+
+    for t in range(tiles):
+
+        def wait_pot(k, _):
+            source = fellow(k)
+            pot_copy(t, source, source).wait_recv()
+            return 0
+
+        lax.fori_loop(1, near, wait_pot, 0)
+
+        def advance(w, _):
+            orbit = orb_ref[w].reshape(width, orb_ref.shape[-1])
+            moved = jnp.dot(recv[t, w], orbit, preferred_element_type=jnp.float32)
+            rows = pl.ds(home, near)
+            old = orb_ref[w, rows, t].astype(jnp.float32)
+            out_ref[w, rows, t] = (old + moved.reshape(old.shape)).astype(jnp.bfloat16)
+            return 0
+
+        lax.fori_loop(0, owned, advance, 0)
+
+    def drain(k, _):
+        peer = peer_of(k)
+        remote(part.at[peer], part_in.at[peer], part_send.at[peer], part_recv.at[peer], peer).wait_send()
+        remote(fields_own, fields_in.at[peer], field_send.at[peer], field_recv.at[peer], peer).wait_send()
+        return 0
+
+    lax.fori_loop(1, n, drain, 0)
+
+    def drain_pot(k, _):
+        for t in range(tiles):
+            pot_copy(t, fellow(k), mine_at).wait_send()
+        return 0
+
+    lax.fori_loop(1, near, drain_pot, 0)
+    for w in range(owned):
+        host(w).wait_send()
+        for oz in range(planes):
+            slot = column(oz)
+
+            @pl.when(depth < planes - 1)
+            def _():
+                guest_copy(slot, w, relay_send.at[0, oz, w], outward).wait_send()
+
+            guest_copy(slot, w, relay_send.at[1, oz, w], beside).wait_send()
+            guest_copy(slot, w, relay_send.at[2, oz, w], partner).wait_send()
+            guest_copy(oz * PLANE + across, w, pass_send.at[oz, w], partner).wait_send()
+
+    def collect(slot, _):
+        for w in range(owned):
+            done_copy(slot, w).wait_send()
+            remote(
+                done.at[slot, w], out_ref.at[w, away + slot], done_send.at[slot, w], done_recv.at[slot, w], away + slot
+            ).wait_recv()
+        return 0
+
+    lax.fori_loop(0, near, collect, 0)
+
+
 def on_device(n, chol_full, chol_half, green, gauss, orbitals):
     walkers, local_rows, nocc = green.shape
     owned, width, _ = orbitals.shape
@@ -196,8 +475,23 @@
     hbm = pl.BlockSpec(memory_space=pl.ANY)
     dma = pltpu.SemaphoreType.DMA
     split = (owned, n, tiles, TILE, nocc)
+    near = n // 2
+    guests = near * orbitals.size * orbitals.dtype.itemsize
+    relayed = n % (2 * PLANE) == 0 and guests <= GUEST_LIMIT
+    peers = near if relayed else n
+    extra, extra_sems = [], []
+    if relayed:
+        planes = near // PLANE
+        extra = [
+            pltpu.VMEM((near,) + split, jnp.bfloat16),
+            pltpu.VMEM((near, owned, tiles, TILE, nocc), jnp.bfloat16),
+        ]
+        extra_sems = [
+            dma((owned,)), dma((near, owned)), dma((3, planes, owned)), dma((planes, owned)),
+            dma((near, owned)), dma((near, owned)),
+        ]
     moved, logs = pl.pallas_call(
-        functools.partial(kernel, n),
+        functools.partial(relay_kernel if relayed else direct_kernel, n),
         out_shape=(
             jax.ShapeDtypeStruct(split, jnp.bfloat16),
             jax.ShapeDtypeStruct((owned, LANES), jnp.float32),
@@ -213,9 +507,10 @@
             pltpu.VMEM((owned, vectors), jnp.float32),
             pltpu.VMEM((n, owned, vectors), jnp.float32),
             pltpu.VMEM((tiles, walkers, TILE, width), jnp.bfloat16),
-            pltpu.VMEM((tiles, owned, n * TILE, width), jnp.bfloat16),
+            pltpu.VMEM((tiles, owned, peers * TILE, width), jnp.bfloat16),
+            *extra,
             dma((tiles,)), dma((2,)), dma((n,)), dma((n,)), dma((n,)), dma((n,)),
-            dma((tiles, n)), dma((tiles, n)),
+            dma((tiles, peers)), dma((tiles, peers)), *extra_sems,
         ],
         compiler_params=pltpu.CompilerParams(
             collective_id=0, has_side_effects=True, vmem_limit_bytes=60 << 20

time: 215 us -> 254 us (1.18)
  the two profiles are of different devices: /device:TPU:13 before, /device:TPU:1 now
where the time goes in v2:
time: 254 us
  Pallas kernels  249 us (98%)
  local copies, waits for them, and re-layouts  4.36 us (2%)
    pallas_call x1, Pallas kernels, on_device(): pl.pallas_call(functools.partial(relay_kernel if relayed else direct_kern...  249 us

profile of v2, /device:TPU:1, one launch (start us, length us, event | category | flops | bytes accessed | tf_op | source)
XLA Modules:
  0.0 253.7 jit_solution(7061205031700900750)
XLA Ops:
  0.6 248.7 %shard_map.68 = (bf16[4,16,4,16,256]{4,3,2,1,0:T(8,128)(2,1)}, f32[4,128]{1,0:T(4,128)}) custom-call(bf16[128,64,1024]{2,1,0:T(8,128)(2,1)} %chol_hbm.1, bf16[128,64,256]{2,1,0:T(8,128)(2,1)} %half_hbm.1, bf16[64,64,256]{2,1,0:T(8,128)(2,1)} %green_hbm.1, f32[16,4,128]{2,1,0:T(4,128)} %bitcast.5, bf16[4,16,4,16,256]{4,3,2,1,0:T(8,128)(2,1)} %bitcast.3), custom_call_target="tpu_custom_call" | custom-call | tf_op jit(solution)/shard_map/pallas_call | solution.py:493
  249.4 1.3 slice_reduce_fusion
  250.7 3.0 %copy.8 = bf16[4,1024,256]{2,1,0:T(8,128)(2,1)} copy(bf16[4,1024,256]{2,1,0:T(8,128)(2,1)} %bitcast.4) | data formatting | bytes 4194304

commit v3 on v2

--- a/solution.py
+++ b/solution.py
@@ -192,9 +192,9 @@
 def relay_kernel(
     n, chol_hbm, half_hbm, green_hbm, gauss_ref, orb_ref,
     out_ref, log_ref,
-    chol, half, green, part, part_in, fields_own, fields_in, send, recv, guest, done,
+    chol, half, green, part, part_in, fields_own, fields_in, send, recv, guest, done, hop,
     load_sem, aux_sem, part_send, part_recv, field_send, field_recv, pot_send, pot_recv,
-    own_send, guest_recv, relay_send, pass_send, done_send, done_recv,
+    own_send, guest_recv, relay_send, pass_send, done_send, done_recv, hop_send, hop_recv,
 ):
     me = lax.axis_index("chol")
     owned = part.shape[1]
@@ -300,6 +300,7 @@
     entry = away + (1 - upper) * 0 + upper * (near - PLANE) + seat
     depth = upper * (mine_at // PLANE) + (1 - upper) * (planes - 1 - mine_at // PLANE)
     outward = lax.rem(me + n + (2 * upper - 1) * PLANE, n)
+    inward = lax.rem(me + n - (2 * upper - 1) * PLANE, n)
     partner = me + 1 - 2 * lax.rem(me, 2)
     beside = me - seat + across
 
@@ -309,11 +310,34 @@
     def guest_copy(slot, w, sem, to):
         return remote(guest.at[slot, w], guest.at[slot, w], sem, guest_recv.at[slot, w], to)
 
+    inner = depth == 0
+    outer = depth > 0
+    behind = lax.rem(outward, near)
+
     def host(w):
         return remote(orb_ref.at[w], guest.at[mine_at, w], own_send.at[w], guest_recv.at[mine_at, w], entry)
 
-    for w in range(owned):
-        host(w).start()
+    def lift(w):
+        return remote(orb_ref.at[w], hop.at[w], own_send.at[w], hop_recv.at[w], inward)
+
+    def onward(w):
+        return remote(hop.at[w], guest.at[behind, w], hop_send.at[w], guest_recv.at[behind, w], entry)
+
+    @pl.when(inner)
+    def _():
+        for w in range(owned):
+            host(w).start()
+
+    @pl.when(outer)
+    def _():
+        for w in range(owned):
+            lift(w).start()
+
+    def forward(w):
+        @pl.when(inner)
+        def _():
+            lift(w).wait_recv()
+            onward(w).start()
 
     def fill(t):
         loads[t].wait()
@@ -347,26 +371,29 @@
 
         lax.fori_loop(1, near, step, 0)
 
-    def column(oz):
-        return oz * PLANE + seat
-
-    def relay(w):
-        for oz in range(planes):
-            slot = column(oz)
-            guest_copy(slot, w, own_send.at[w], partner).wait_recv()
-
-            @pl.when(depth < planes - 1)
-            def _():
-                guest_copy(slot, w, relay_send.at[0, oz, w], outward).start()
-
-            guest_copy(slot, w, relay_send.at[1, oz, w], beside).start()
-            guest_copy(slot, w, relay_send.at[2, oz, w], partner).start()
-
-    def hand_over(w):
-        for oz in range(planes):
-            slot = oz * PLANE + across
-            guest_copy(slot, w, own_send.at[w], partner).wait_recv()
-            guest_copy(slot, w, pass_send.at[oz, w], partner).start()
+    first = away // near
+
+    def block(s):
+        oz = s // owned
+        return (oz + (1 - 2 * oz) * (1 - first), s % owned)
+
+    def relay(s):
+        oz, w = block(s)
+        slot = oz * PLANE + seat
+        guest_copy(slot, w, own_send.at[w], partner).wait_recv()
+
+        @pl.when(inner)
+        def _():
+            guest_copy(slot, w, relay_send.at[0, s], outward).start()
+
+        guest_copy(slot, w, relay_send.at[1, s], beside).start()
+        guest_copy(slot, w, relay_send.at[2, s], partner).start()
+
+    def hand_over(s):
+        oz, w = block(s)
+        slot = oz * PLANE + across
+        guest_copy(slot, w, own_send.at[w], partner).wait_recv()
+        guest_copy(slot, w, pass_send.at[s], partner).start()
 
     def done_copy(slot, w):
         return remote(
@@ -381,33 +408,35 @@
         done[slot, w] = (old + moved.reshape(old.shape)).astype(jnp.bfloat16)
         done_copy(slot, w).start()
 
-    def serve_column(w, j, wait):
-        for oz in range(planes):
-            slot = oz * PLANE + j
-            if wait:
-                guest_copy(slot, w, own_send.at[w], partner).wait_recv()
-            serve(slot, w)
-
+    def serve_block(s, j, wait):
+        oz, w = block(s)
+        slot = oz * PLANE + j
+        if wait:
+            guest_copy(slot, w, own_send.at[w], partner).wait_recv()
+        serve(slot, w)
+
+    steps = planes * owned
+    early = tiles // 2
     for t in range(tiles):
         fill(t)
-        if t == 0:
-            push(0)
-    for w in range(owned + 1):
-        if w < owned:
-            relay(w)
-        if w == owned - 1 or (w < owned and w + 1 >= tiles):
-            for t in range(w + 1, tiles):
+        if t < early:
+            push(t)
+    for s in range(steps + 2):
+        if s < owned:
+            forward(s)
+        if s < steps:
+            relay(s)
+        if s == steps - 1:
+            for t in range(early, tiles):
                 push(t)
-        elif w < owned:
-            push(w + 1)
-        if w > 0:
-            hand_over(w - 1)
-        if w < owned:
-            serve_column(w, seat, False)
-            serve_column(w, swap(seat), True)
-        if w > 0:
-            serve_column(w - 1, across, False)
-            serve_column(w - 1, swap(across), True)
+        if 0 < s <= steps:
+            hand_over(s - 1)
+        if s < steps:
+            serve_block(s, seat, False)
+            serve_block(s, swap(seat), True)
+        if s > 1:
+            serve_block(s - 2, across, False)
+            serve_block(s - 2, swap(across), True)
 
     for t in range(tiles):
 
@@ -444,16 +473,22 @@
     lax.fori_loop(1, near, drain_pot, 0)
     for w in range(owned):
         host(w).wait_send()
-        for oz in range(planes):
-            slot = column(oz)
-
-            @pl.when(depth < planes - 1)
-            def _():
-                guest_copy(slot, w, relay_send.at[0, oz, w], outward).wait_send()
-
-            guest_copy(slot, w, relay_send.at[1, oz, w], beside).wait_send()
-            guest_copy(slot, w, relay_send.at[2, oz, w], partner).wait_send()
-            guest_copy(oz * PLANE + across, w, pass_send.at[oz, w], partner).wait_send()
+
+        @pl.when(inner)
+        def _():
+            onward(w).wait_send()
+
+    for s in range(steps):
+        oz, w = block(s)
+        slot = oz * PLANE + seat
+
+        @pl.when(inner)
+        def _():
+            guest_copy(slot, w, relay_send.at[0, s], outward).wait_send()
+
+        guest_copy(slot, w, relay_send.at[1, s], beside).wait_send()
+        guest_copy(slot, w, relay_send.at[2, s], partner).wait_send()
+        guest_copy(slot, w, pass_send.at[s], partner).wait_send()
 
     def collect(slot, _):
         for w in range(owned):
@@ -477,7 +512,7 @@
     split = (owned, n, tiles, TILE, nocc)
     near = n // 2
     guests = near * orbitals.size * orbitals.dtype.itemsize
-    relayed = n % (2 * PLANE) == 0 and guests <= GUEST_LIMIT
+    relayed = n == 4 * PLANE and guests <= GUEST_LIMIT
     peers = near if relayed else n
     extra, extra_sems = [], []
     if relayed:
@@ -485,10 +520,11 @@
         extra = [
             pltpu.VMEM((near,) + split, jnp.bfloat16),
             pltpu.VMEM((near, owned, tiles, TILE, nocc), jnp.bfloat16),
+            pltpu.VMEM(split, jnp.bfloat16),
         ]
         extra_sems = [
-            dma((owned,)), dma((near, owned)), dma((3, planes, owned)), dma((planes, owned)),
-            dma((near, owned)), dma((near, owned)),
+            dma((owned,)), dma((near, owned)), dma((3, planes * owned)), dma((planes * owned,)),
+            dma((near, owned)), dma((near, owned)), dma((owned,)), dma((owned,)),
         ]
     moved, logs = pl.pallas_call(
         functools.partial(relay_kernel if relayed else direct_kernel, n),

time: 254 us -> 207 us (0.81)
  Pallas kernels: 249 us -> 202 us
    pallas_call x1, Pallas kernels: 249 us -> 202 us  [on_device(): pl.pallas_call(functools.partial(relay_kernel if relayed else direct_kern...]
where the time goes in v3:
time: 207 us
  Pallas kernels  202 us (98%)
  local copies, waits for them, and re-layouts  4.36 us (2%)
    pallas_call x1, Pallas kernels, on_device(): pl.pallas_call(functools.partial(relay_kernel if relayed else direct_kern...  202 us

profile of v3, /device:TPU:1, one launch (start us, length us, event | category | flops | bytes accessed | tf_op | source)
XLA Modules:
  0.0 207.1 jit_solution(8951414544406284000)
XLA Ops:
  0.6 202.1 %shard_map.68 = (bf16[4,16,4,16,256]{4,3,2,1,0:T(8,128)(2,1)}, f32[4,128]{1,0:T(4,128)}) custom-call(bf16[128,64,1024]{2,1,0:T(8,128)(2,1)} %chol_hbm.1, bf16[128,64,256]{2,1,0:T(8,128)(2,1)} %half_hbm.1, bf16[64,64,256]{2,1,0:T(8,128)(2,1)} %green_hbm.1, f32[16,4,128]{2,1,0:T(4,128)} %bitcast.5, bf16[4,16,4,16,256]{4,3,2,1,0:T(8,128)(2,1)} %bitcast.3), custom_call_target="tpu_custom_call" | custom-call | tf_op jit(solution)/shard_map/pallas_call | solution.py:529
  202.8 1.3 slice_reduce_fusion
  204.1 3.0 %copy.8 = bf16[4,1024,256]{2,1,0:T(8,128)(2,1)} copy(bf16[4,1024,256]{2,1,0:T(8,128)(2,1)} %bitcast.4) | data formatting | bytes 4194304

commit v4 on v3

--- a/solution.py
+++ b/solution.py
@@ -416,7 +416,7 @@
         serve(slot, w)
 
     steps = planes * owned
-    early = tiles // 2
+    early = tiles - 1
     for t in range(tiles):
         fill(t)
         if t < early:

time: 207 us -> 204 us (0.986)
  Pallas kernels: 202 us -> 198 us
    pallas_call x1, Pallas kernels: 202 us -> 198 us  [on_device(): pl.pallas_call(functools.partial(relay_kernel if relayed else direct_kern...]
where the time goes in v4:
time: 204 us; the launch traced here: 203 us
  Pallas kernels  198 us (97%)
  local copies, waits for them, and re-layouts  4.36 us (2%)
    pallas_call x1, Pallas kernels, on_device(): pl.pallas_call(functools.partial(relay_kernel if relayed else direct_kern...  198 us

profile of v4, /device:TPU:1, one launch (start us, length us, event | category | flops | bytes accessed | tf_op | source)
XLA Modules:
  0.0 203.5 jit_solution(602266556046832851)
XLA Ops:
  0.6 198.5 %shard_map.68 = (bf16[4,16,4,16,256]{4,3,2,1,0:T(8,128)(2,1)}, f32[4,128]{1,0:T(4,128)}) custom-call(bf16[128,64,1024]{2,1,0:T(8,128)(2,1)} %chol_hbm.1, bf16[128,64,256]{2,1,0:T(8,128)(2,1)} %half_hbm.1, bf16[64,64,256]{2,1,0:T(8,128)(2,1)} %green_hbm.1, f32[16,4,128]{2,1,0:T(4,128)} %bitcast.5, bf16[4,16,4,16,256]{4,3,2,1,0:T(8,128)(2,1)} %bitcast.3), custom_call_target="tpu_custom_call" | custom-call | tf_op jit(solution)/shard_map/pallas_call | solution.py:529
  199.1 1.3 slice_reduce_fusion
  200.4 3.0 %copy.8 = bf16[4,1024,256]{2,1,0:T(8,128)(2,1)} copy(bf16[4,1024,256]{2,1,0:T(8,128)(2,1)} %bitcast.4) | data formatting | bytes 4194304
